TPU v7x, 32 devices: a whole 2x2x4 slice. The times are simulated.
32 devices in a mesh: energy: 8 (over y, x, core), kpt: 4 (over z).
Axes of the slice: x: 2, y: 2, z: 4, core: 2. Of those that a mesh axis runs over, the one named last changes fastest.
Arguments:
- density: bfloat16 [32, 4, 64, 3072], P('energy', 'kpt'), may hold values from -6 to 6
- quad_weights: float32 [32, 4], P('energy', 'kpt'), may hold values from 0.044194173 to 0.17677669
- orbital_cells: int32 [64, 3072], replicated, may hold values from 0 to 131071
- fixed_charge: float32 [512, 64, 256], P('energy', 'kpt'), may hold values from -16 to 16
- gate_mask: int32 [512, 64, 256], P('energy', 'kpt'), may hold values 0 or 1
- gate_voltage: float32 [512], P('energy'), may hold values from -1 to 1
Outputs:
- potential: float32 [512, 64, 256], P('energy', 'kpt')
- band_shift: float32 [32, 4, 64], P('energy', 'kpt')
Inputs may be any that keep to these rules, and one draw needn't show every extreme that they name: `orbital_cells`: each entry is s * 64 * 256 + y * 256 + z, a cell of one of the layer's 8 planes.
All inputs are finite; a program needn't handle non-finite values. No bound on the sum of `gate_mask` on one device may be relied on, other than what follows from the above.
Results may differ from a plain program's by a relative error of at most 0.0003.
Values sent between devices are 32-bit elements; how exact they have to be, the bound alone decides.
A program may use at most 64 MiB of HBM per device.

v0:
```python
import jax
import jax.numpy as jnp
from jax import lax
from jax.sharding import PartitionSpec as P

LAYER_DEV = 8
SUB = 8
ITERS = 2
PENALTY = 4.0


def with_halo(block, sides, width):
    for axis, dim in sides:
        count = lax.axis_size(axis)
        forward = [(i, i + 1) for i in range(count - 1)]
        backward = [(target, source) for source, target in forward]
        low = lax.ppermute(
            lax.slice_in_dim(block, block.shape[dim] - width, None, axis=dim), axis, forward
        )
        high = lax.ppermute(lax.slice_in_dim(block, 0, width, axis=dim), axis, backward)
        block = jnp.concatenate([low, block, high], axis=dim)
    return block


def operate(values_field, diagonal):
    padded = with_halo(values_field, (("energy", 0), ("kpt", 1)), 1)
    padded = jnp.pad(padded, ((0, 0), (0, 0), (1, 1)))
    beside = padded[2:, 1:-1, 1:-1] + padded[:-2, 1:-1, 1:-1]
    beside = beside + padded[1:-1, 2:, 1:-1] + padded[1:-1, :-2, 1:-1]
    beside = beside + padded[1:-1, 1:-1, 2:] + padded[1:-1, 1:-1, :-2]
    return diagonal * values_field - beside


def paired_sums(residual, image):
    return lax.psum((jnp.sum(residual * residual), jnp.sum(residual * image)), ("energy", "kpt"))


def window_index(map_rows, kpt_index, planes, cross_y, width_y, depth_z):
    section = cross_y * depth_z
    within = map_rows % section
    column = within // depth_z - kpt_index * width_y
    inside = (column >= 0) & (column < width_y)
    layer_rows = lax.broadcasted_iota(jnp.int32, map_rows.shape, 0)
    flat_cell = (
        (layer_rows * planes + map_rows // section) * width_y + jnp.clip(column, 0, width_y - 1)
    ) * depth_z + within % depth_z
    return (flat_cell, inside)


def per_device(density, quad_weights, orbital_cells, fixed_charge, gate_mask, gate_voltage):
    planes_dev, width_y, depth_z = fixed_charge.shape
    kpt_index = lax.axis_index("kpt")
    cross_y = width_y * lax.axis_size("kpt")
    occupancy = jnp.einsum(
        "ek,eklo->lo", quad_weights, density.astype(jnp.float32), precision=lax.Precision.HIGHEST
    )
    partial_rows = lax.psum_scatter(occupancy, "energy", scatter_dimension=0, tiled=True)
    slab_occupancy = lax.psum(partial_rows, "kpt")
    slab_cells = lax.dynamic_slice_in_dim(
        orbital_cells, lax.axis_index("energy") * LAYER_DEV, LAYER_DEV, 0
    )
    flat_cell, inside = window_index(slab_cells, kpt_index, SUB, cross_y, width_y, depth_z)
    deposit = jax.ops.segment_sum(
        jnp.where(inside, slab_occupancy, 0.0).reshape(-1),
        flat_cell.reshape(-1),
        num_segments=planes_dev * width_y * depth_z,
    )
    charge = deposit.reshape(planes_dev, width_y, depth_z)
    gated = gate_mask.astype(jnp.float32)
    diagonal = 6.0 + PENALTY * gated
    right_side = fixed_charge - charge + PENALTY * gated * gate_voltage[:, None, None]
    potential = jnp.zeros_like(right_side)
    residual = right_side
    image = operate(residual, diagonal)
    norm_now, product = paired_sums(residual, image)
    alpha = norm_now / product
    direction = residual
    along = image
    for sweep_index in range(ITERS):
        potential = potential + alpha * direction
        residual = residual - alpha * along
        if sweep_index + 1 < ITERS:
            image = operate(residual, diagonal)
            norm_next, product = paired_sums(residual, image)
            ratio = norm_next / norm_now
            alpha = norm_next / (product - ratio * norm_next / alpha)
            direction = residual + ratio * direction
            along = image + ratio * along
            norm_now = norm_next
    local_values = jnp.where(inside, jnp.take(potential.reshape(-1), flat_cell), 0.0)
    orbital_potential = lax.psum(local_values, "kpt")
    factor = density.shape[3] ** (-0.5)
    block = density.astype(jnp.float32)
    band_shift = (
        jnp.einsum(
            "eklo,lo->ekl",
            block,
            lax.all_gather(orbital_potential, "energy", axis=0, tiled=True),
            precision=lax.Precision.HIGHEST,
        )
        * factor
    )
    return (potential, band_shift)


def solution(mesh):
    in_specs = (
        P("energy", "kpt", None, None),
        P("energy", "kpt"),
        P(),
        P("energy", "kpt", None),
        P("energy", "kpt", None),
        P("energy"),
    )
    out_specs = (P("energy", "kpt", None), P("energy", "kpt", None))
    return jax.shard_map(
        per_device, mesh=mesh, in_specs=in_specs, out_specs=out_specs, check_vma=False
    )
```

profile of v0, /device:TPU:0, one launch (start us, length us, event | category | flops | bytes accessed | tf_op | source)
XLA Modules:
  0.0 549.4 jit_solution(11437265235670384205)
XLA Ops:
  7.2 1.4 copy-done
  8.6 3.8 fusion.3
  14.6 36.6 %reduce-scatter.2.cloned.1.call-done = f32[8,3072]{1,0:T(8,128)} async-done(((f32[64,3072]{1,0:T(8,128)}), f32[8,3072]{1,0:T(8,128)}) %reduce-scatter.2.cloned.1.call-update) | async-done | bytes 98320 | tf_op jit(solution)/shard_map/reduce_scatter | solution.py:57
  51.3 36.7 %all-reduce.7.cloned.1.call-done = f32[8,3072]{1,0:T(8,128)} async-done(((f32[8,3072]{1,0:T(8,128)}), f32[8,3072]{1,0:T(8,128)}) %all-reduce.7.cloned.1.call-update) | async-done | bytes 98320 | tf_op jit(solution)/shard_map/psum | solution.py:58
  89.1 128.7 %scatter_custom_fusion = f32[262144]{0:T(1024)S(1)} fusion(s32[24576]{0:T(1024)S(1)} %bitcast.33, f32[24576]{0:T(1024)S(1)} %bitcast.34, f32[]{:T(128)} %constant.72.clone.1), kind=kCustom, calls=%fused_computation.56 | custom fusion | flops 24576 | bytes 1048580 | tf_op jit(solution)/shard_map/scatter-add | solution.py:63
  219.1 2.1 multiply_add_fusion.2
  222.5 1.4 collective-permute-start
  223.9 3.5 collective-permute-done
  228.8 4.5 collective-permute-start.3
  233.9 1.5 collective-permute-done.3
  236.7 2.6 multiply_reduce_fusion.1
  239.3 42.2 %all-reduce.3 = (f32[]{:T(128)}, f32[]{:T(128)}) all-reduce(f32[]{:T(128)} %get-tuple-element.7, f32[]{:T(128)} %get-tuple-element.6), channel_id=1, replica_groups=mesh['energy'=8,'kpt'=4] {'energy','kpt'}, use_global_device_ids=true, to_apply=%region_4.5 | all-reduce | flops 2 | bytes 16 | tf_op jit(solution)/shard_map/psum | solution.py:35
  282.8 1.5 multiply_subtract_fusion
  286.9 4.2 collective-permute-done.4
  291.3 1.4 collective-permute-start.6
  292.8 4.5 collective-permute-start.7
  297.8 1.5 collective-permute-done.7
  300.6 1.7 fusion.7
  302.3 42.7 %all-reduce.2 = (f32[]{:T(128)}, f32[]{:T(128)}) all-reduce(f32[]{:T(128)} %get-tuple-element.5, f32[]{:T(128)} %get-tuple-element.4), channel_id=1, replica_groups=mesh['energy'=8,'kpt'=4] {'energy','kpt'}, use_global_device_ids=true, to_apply=%region_8.9 | all-reduce | flops 2 | bytes 16 | tf_op jit(solution)/shard_map/psum | solution.py:35
  349.4 1.5 multiply_add_fusion
  352.4 135.5 %gather_fusion = f32[24576]{0:T(1024)S(1)} fusion(f32[262144]{0:T(1024)S(1)} %bitcast.27, s32[24576]{0:T(1024)S(1)} %broadcast_clamp_fusion), kind=kCustom, calls=%fused_computation | custom fusion | bytes 294912 | tf_op jit(solution)/shard_map/jit(_take)/gather | solution.py:90
  488.7 35.5 %all-reduce.9.cloned.1.call-done = f32[8,3072]{1,0:T(8,128)} async-done(((f32[8,3072]{1,0:T(8,128)}), f32[8,3072]{1,0:T(8,128)}) %all-reduce.9.cloned.1.call-update) | async-done | bytes 98320 | tf_op jit(solution)/shard_map/psum | solution.py:91
  524.2 10.7 %all_gather.3 = f32[64,3072]{1,0:T(8,128)S(1)} all-gather(f32[8,3072]{1,0:T(8,128)} %all-reduce.9.cloned.1.call-done), channel_id=1, replica_groups=mesh['energy'=8,'kpt'=4] {'energy'}, dimensions={0}, use_global_device_ids=true | all-gather | bytes 884736 | tf_op jit(solution)/shard_map/all_gather | solution.py:98
  534.8 7.3 %fusion.1 = f32[64,1,4]{2,1,0:T(1,128)S(1)} fusion(bf16[4,64,3072]{2,1,0:T(8,128)(2,1)S(1)} %bitcast.26, f32[64,3072,1]{1,0,2:T(8,128)S(1)} %bitcast.31), kind=kOutput, calls=%fused_computation.13 | convolution fusion | flops 9437184 | bytes 2360320 | tf_op jit(solution)/shard_map/eklo,lo->ekl/dot_general | solution.py:95
  (54 shorter events, 16.5 us)
Async XLA Ops:
  7.2 1.4 copy-start
  7.2 44.0 %reduce-scatter.2.cloned.1.call-start = ((), (), s32[]{:S(2)}) async-start(), calls=%async_computation.1 | async-start | bytes 884736 | tf_op jit(solution)/shard_map/reduce_scatter | solution.py:57
  8.6 42.7 %copy-start.5 = (f32[64]{0:T(128)S(1)}, f32[64]{0:T(128)}, u32[]{:S(2)}) copy-start(f32[64]{0:T(128)} %param.11) | copy-start | bytes 772
  13.4 74.6 %all-reduce.7.cloned.1.call-start = ((), (), s32[]{:S(2)}) async-start(), calls=%async_computation.2 | async-start | bytes 196608 | tf_op jit(solution)/shard_map/psum | solution.py:58
  51.2 472.9 %all-reduce.9.cloned.1.call-start = ((), (), s32[]{:S(2)}) async-start(), calls=%async_computation.3 | async-start | bytes 196608 | tf_op jit(solution)/shard_map/psum | solution.py:91
  221.2 2.7 collective-permute-start.1
  222.5 14.2 %copy-start.2 = (s32[64,16,256]{2,1,0:T(8,128)S(1)}, s32[64,16,256]{2,1,0:T(8,128)}, u32[]{:S(2)}) copy-start(s32[64,16,256]{2,1,0:T(8,128)} %param.10) | copy-start | bytes 3145732
  222.5 4.9 collective-permute-start
  227.5 6.2 %collective-permute-start.2 = (f32[66,1,256]{2,0,1:T(8,128)S(1)}, f32[66,1,256]{2,0,1:T(8,128)S(1)}, u32[]{:S(2)}, u32[]{:S(2)}) collective-permute-start(f32[66,1,256]{2,0,1:T(8,128)S(1)} %copy.11), channel_id=1, source_target_pairs={{1,0},{2,1},{3,2},{5,4},{6,5},{7,6},{9,8},{10,9},{11,10},{13,12},{... | collective-permute-start | bytes 202760 | tf_op jit(solution)/shard_map/ppermute | solution.py:20
  228.8 6.5 %collective-permute-start.3 = (f32[66,1,256]{2,0,1:T(8,128)S(1)}, f32[66,1,256]{2,0,1:T(8,128)S(1)}, u32[]{:S(2)}, u32[]{:S(2)}) collective-permute-start(f32[66,1,256]{2,0,1:T(8,128)S(1)} %copy.13), channel_id=1, source_target_pairs={{0,1},{1,2},{2,3},{4,5},{5,6},{6,7},{8,9},{9,10},{10,11},{12,13},{... | collective-permute-start | bytes 202760 | tf_op jit(solution)/shard_map/ppermute | solution.py:17
  284.3 16.3 %copy-start.1 = (f32[64,16,256]{2,1,0:T(8,128)}, f32[64,16,256]{2,1,0:T(8,128)S(1)}, u32[]{:S(2)}) copy-start(f32[64,16,256]{2,1,0:T(8,128)S(1)} %multiply_subtract_fusion) | copy-start | bytes 3145732
  284.3 2.6 collective-permute-start.5
  285.6 5.6 %collective-permute-start.4 = (f32[1,16,256]{2,1,0:T(8,128)S(1)}, f32[1,16,256]{2,1,0:T(8,128)S(1)}, u32[]{:S(2)}, u32[]{:S(2)}) collective-permute-start(f32[1,16,256]{2,1,0:T(8,128)S(1)} %get-tuple-element.23), channel_id=1, source_target_pairs={{4,0},{8,4},{12,8},{16,12},{20,16},{24,20},{28,24},{5,1},{9,5},{13... | collective-permute-start | bytes 49160 | tf_op jit(solution)/shard_map/ppermute | solution.py:20
  291.3 9.3 %copy-start.3 = (s32[64,16,256]{2,1,0:T(8,128)S(1)}, s32[64,16,256]{2,1,0:T(8,128)}, u32[]{:S(2)}) copy-start(s32[64,16,256]{2,1,0:T(8,128)} %param.10) | copy-start | bytes 3145732
  291.3 6.4 %collective-permute-start.6 = (f32[66,1,256]{2,0,1:T(8,128)S(1)}, f32[66,1,256]{2,0,1:T(8,128)S(1)}, u32[]{:S(2)}, u32[]{:S(2)}) collective-permute-start(f32[66,1,256]{2,0,1:T(8,128)S(1)} %copy.17), channel_id=1, source_target_pairs={{1,0},{2,1},{3,2},{5,4},{6,5},{7,6},{9,8},{10,9},{11,10},{13,12},{... | collective-permute-start | bytes 202760 | tf_op jit(solution)/shard_map/ppermute | solution.py:20
  292.8 6.5 %collective-permute-start.7 = (f32[66,1,256]{2,0,1:T(8,128)S(1)}, f32[66,1,256]{2,0,1:T(8,128)S(1)}, u32[]{:S(2)}, u32[]{:S(2)}) collective-permute-start(f32[66,1,256]{2,0,1:T(8,128)S(1)} %copy.19), channel_id=1, source_target_pairs={{0,1},{1,2},{2,3},{4,5},{5,6},{6,7},{8,9},{9,10},{10,11},{12,13},{... | collective-permute-start | bytes 202760 | tf_op jit(solution)/shard_map/ppermute | solution.py:17
  350.9 1.0 copy-start.4
Sparse Core Ops, SparseCore 0:
  13.5 37.6 reduce-scatter.1
  53.5 34.4 all-reduce.6
  488.8 35.3 all-reduce.8
where the time goes:
time: 550 us; the launch traced here: 549 us
  other arithmetic  144 us (26%)
  local copies, waits for them, and re-layouts  141 us (26%)
  waiting for transfers between devices  120 us (22%)
  blocking collectives  95.6 us (17%)
  between operations  19.7 us (4%)
  starting transfers between devices  17.2 us (3%)
  matrix products  11.1 us (2%)
    gather x2, local copies, waits for them, and re-layouts, per_device(): jnp.take(potential.reshape(-1), flat_cell)  136 us
    scatter-add x1, other arithmetic, per_device(): jax.ops.segment_sum(jnp.where(inside, slab_occupancy, 0.0).reshape(-1), f...  129 us
    psum x2, blocking collectives, paired_sums(): lax.psum((jnp.sum(residual * residual), jnp.sum(residual * image)), ('ene...  84.9 us
    psum x1, waiting for transfers between devices, per_device(): slab_occupancy = lax.psum(partial_rows, 'kpt')  36.7 us
    reduce_scatter x1, waiting for transfers between devices, per_device(): lax.psum_scatter(occupancy, 'energy', scatter_dimension=0, tiled=True)  36.6 us
    psum x1, waiting for transfers between devices, per_device(): orbital_potential = lax.psum(local_values, 'kpt')  35.5 us
    ppermute x4, starting transfers between devices, with_halo(): lax.ppermute(lax.slice_in_dim(block, block.shape[dim] - width, None, axis...  11.7 us
  transfers between devices with their start and end apart: 11, of which 9 were waited for; matrix products, arithmetic and copies ran while one was open for 0% of the time, Pallas kernels for 0%

commit v1 on v0

--- a/solution.py
+++ b/solution.py
@@ -88,7 +88,11 @@
             along = image + ratio * along
             norm_now = norm_next
     local_values = jnp.where(inside, jnp.take(potential.reshape(-1), flat_cell), 0.0)
-    orbital_potential = lax.psum(local_values, "kpt")
+    orbital_potential = local_values
+    for hop in (1, 2):
+        orbital_potential = orbital_potential + lax.ppermute(
+            orbital_potential, "kpt", [(dev, dev ^ hop) for dev in range(4)]
+        )
     factor = density.shape[3] ** (-0.5)
     block = density.astype(jnp.float32)
     band_shift = (

time: 550 us -> 527 us (0.958)
  waiting for transfers between devices: 120 us -> 92.6 us
    psum x1 -> x0, waiting for transfers between devices: 35.5 us -> none  [per_device(): orbital_potential = lax.psum(local_values, 'kpt')]
    ppermute x0 -> x2, waiting for transfers between devices: none -> 7.8 us  [per_device(): lax.ppermute(orbital_potential, 'kpt', [(dev, dev ^ hop) for dev in range...]
  transfers between devices with their start and end apart: 11 -> 12, of which waited for: 9 -> 10; matrix products, arithmetic and copies ran while one was open for 0% -> 0% of each run, Pallas kernels for 0% -> 0%
where the time goes in v1:
time: 527 us; the launch traced here: 526 us
  other arithmetic  144 us (27%)
  local copies, waits for them, and re-layouts  141 us (27%)
  blocking collectives  96.3 us (18%)
  waiting for transfers between devices  92.6 us (18%)
  starting transfers between devices  20.7 us (4%)
  between operations  20.1 us (4%)
  matrix products  11.1 us (2%)
    gather x2, local copies, waits for them, and re-layouts, per_device(): jnp.take(potential.reshape(-1), flat_cell)  136 us
    scatter-add x1, other arithmetic, per_device(): jax.ops.segment_sum(jnp.where(inside, slab_occupancy, 0.0).reshape(-1), f...  129 us
    psum x2, blocking collectives, paired_sums(): lax.psum((jnp.sum(residual * residual), jnp.sum(residual * image)), ('ene...  84.9 us
    psum x1, waiting for transfers between devices, per_device(): slab_occupancy = lax.psum(partial_rows, 'kpt')  36.7 us
    reduce_scatter x1, waiting for transfers between devices, per_device(): lax.psum_scatter(occupancy, 'energy', scatter_dimension=0, tiled=True)  36.6 us
    ppermute x4, starting transfers between devices, with_halo(): lax.ppermute(lax.slice_in_dim(block, block.shape[dim] - width, None, axis...  11.7 us
    all_gather x1, blocking collectives, per_device(): lax.all_gather(orbital_potential, 'energy', axis=0, tiled=True)  11.4 us
  transfers between devices with their start and end apart: 12, of which 10 were waited for; matrix products, arithmetic and copies ran while one was open for 0% of the time, Pallas kernels for 0%

profile of v1, /device:TPU:0, one launch (start us, length us, event | category | flops | bytes accessed | tf_op | source)
XLA Modules:
  0.0 525.7 jit_solution(5177708503255093533)
XLA Ops:
  8.6 3.8 fusion.3
  14.6 36.6 %reduce-scatter.2.cloned.1.call-done = f32[8,3072]{1,0:T(8,128)} async-done(((f32[64,3072]{1,0:T(8,128)}), f32[8,3072]{1,0:T(8,128)}) %reduce-scatter.2.cloned.1.call-update) | async-done | bytes 98320 | tf_op jit(solution)/shard_map/reduce_scatter | solution.py:57
  51.3 36.7 %all-reduce.6.cloned.1.call-done = f32[8,3072]{1,0:T(8,128)} async-done(((f32[8,3072]{1,0:T(8,128)}), f32[8,3072]{1,0:T(8,128)}) %all-reduce.6.cloned.1.call-update) | async-done | bytes 98320 | tf_op jit(solution)/shard_map/psum | solution.py:58
  89.1 128.7 %scatter_custom_fusion = f32[262144]{0:T(1024)S(1)} fusion(s32[24576]{0:T(1024)S(1)} %bitcast.33, f32[24576]{0:T(1024)S(1)} %bitcast.34, f32[]{:T(128)} %constant.72.clone.1), kind=kCustom, calls=%fused_computation.56 | custom fusion | flops 24576 | bytes 1048580 | tf_op jit(solution)/shard_map/scatter-add | solution.py:63
  219.1 2.1 multiply_add_fusion.2
  223.9 3.5 collective-permute-done
  228.8 4.5 collective-permute-start.3
  233.9 1.5 collective-permute-done.3
  236.7 2.7 multiply_reduce_fusion.1
  239.4 42.2 %all-reduce.3 = (f32[]{:T(128)}, f32[]{:T(128)}) all-reduce(f32[]{:T(128)} %get-tuple-element.7, f32[]{:T(128)} %get-tuple-element.6), channel_id=1, replica_groups=mesh['energy'=8,'kpt'=4] {'energy','kpt'}, use_global_device_ids=true, to_apply=%region_4.5 | all-reduce | flops 2 | bytes 16 | tf_op jit(solution)/shard_map/psum | solution.py:35
  282.8 1.5 multiply_subtract_fusion
  287.0 4.2 collective-permute-done.4
  291.4 1.4 collective-permute-start.6
  292.8 4.5 collective-permute-start.7
  297.8 1.5 collective-permute-done.7
  300.7 1.7 fusion.7
  302.3 42.7 %all-reduce.2 = (f32[]{:T(128)}, f32[]{:T(128)}) all-reduce(f32[]{:T(128)} %get-tuple-element.5, f32[]{:T(128)} %get-tuple-element.4), channel_id=1, replica_groups=mesh['energy'=8,'kpt'=4] {'energy','kpt'}, use_global_device_ids=true, to_apply=%region_8.9 | all-reduce | flops 2 | bytes 16 | tf_op jit(solution)/shard_map/psum | solution.py:35
  349.5 1.5 multiply_add_fusion
  352.5 135.5 %gather_fusion = f32[24576]{0:T(1024)S(1)} fusion(f32[262144]{0:T(1024)S(1)} %bitcast.27, s32[24576]{0:T(1024)S(1)} %broadcast_clamp_fusion), kind=kCustom, calls=%fused_computation | custom fusion | bytes 294912 | tf_op jit(solution)/shard_map/jit(_take)/gather | solution.py:90
  489.5 3.3 collective-permute-done.8
  492.8 2.1 collective-permute-start.9
  494.9 4.5 collective-permute-done.9
  499.4 11.4 %all_gather.3 = f32[64,3072]{1,0:T(8,128)S(1)} all-gather(f32[8,3072]{1,0:T(8,128)S(1)} %add.125), channel_id=1, replica_groups=mesh['energy'=8,'kpt'=4] {'energy'}, dimensions={0}, use_global_device_ids=true | all-gather | bytes 884736 | tf_op jit(solution)/shard_map/all_gather | solution.py:102
  510.9 7.3 %fusion.1 = f32[64,1,4]{2,1,0:T(1,128)S(1)} fusion(bf16[4,64,3072]{2,1,0:T(8,128)(2,1)S(1)} %bitcast.26, f32[64,3072,1]{1,0,2:T(8,128)S(1)} %bitcast.31), kind=kOutput, calls=%fused_computation.13 | convolution fusion | flops 9437184 | bytes 2360320 | tf_op jit(solution)/shard_map/eklo,lo->ekl/dot_general | solution.py:99
  (57 shorter events, 20.1 us)
Async XLA Ops:
  7.2 1.4 copy-start
  7.2 44.0 %reduce-scatter.2.cloned.1.call-start = ((), (), s32[]{:S(2)}) async-start(), calls=%async_computation.1 | async-start | bytes 884736 | tf_op jit(solution)/shard_map/reduce_scatter | solution.py:57
  8.6 42.7 %copy-start.5 = (f32[64]{0:T(128)S(1)}, f32[64]{0:T(128)}, u32[]{:S(2)}) copy-start(f32[64]{0:T(128)} %param.11) | copy-start | bytes 772
  13.4 74.6 %all-reduce.6.cloned.1.call-start = ((), (), s32[]{:S(2)}) async-start(), calls=%async_computation.2 | async-start | bytes 196608 | tf_op jit(solution)/shard_map/psum | solution.py:58
  221.2 2.7 collective-permute-start.1
  222.5 14.2 %copy-start.2 = (s32[64,16,256]{2,1,0:T(8,128)S(1)}, s32[64,16,256]{2,1,0:T(8,128)}, u32[]{:S(2)}) copy-start(s32[64,16,256]{2,1,0:T(8,128)} %param.10) | copy-start | bytes 3145732
  222.5 4.9 collective-permute-start
  227.5 6.2 %collective-permute-start.2 = (f32[66,1,256]{2,0,1:T(8,128)S(1)}, f32[66,1,256]{2,0,1:T(8,128)S(1)}, u32[]{:S(2)}, u32[]{:S(2)}) collective-permute-start(f32[66,1,256]{2,0,1:T(8,128)S(1)} %copy.11), channel_id=1, source_target_pairs={{1,0},{2,1},{3,2},{5,4},{6,5},{7,6},{9,8},{10,9},{11,10},{13,12},{... | collective-permute-start | bytes 202760 | tf_op jit(solution)/shard_map/ppermute | solution.py:20
  228.8 6.5 %collective-permute-start.3 = (f32[66,1,256]{2,0,1:T(8,128)S(1)}, f32[66,1,256]{2,0,1:T(8,128)S(1)}, u32[]{:S(2)}, u32[]{:S(2)}) collective-permute-start(f32[66,1,256]{2,0,1:T(8,128)S(1)} %copy.13), channel_id=1, source_target_pairs={{0,1},{1,2},{2,3},{4,5},{5,6},{6,7},{8,9},{9,10},{10,11},{12,13},{... | collective-permute-start | bytes 202760 | tf_op jit(solution)/shard_map/ppermute | solution.py:17
  284.3 16.3 %copy-start.1 = (f32[64,16,256]{2,1,0:T(8,128)}, f32[64,16,256]{2,1,0:T(8,128)S(1)}, u32[]{:S(2)}) copy-start(f32[64,16,256]{2,1,0:T(8,128)S(1)} %multiply_subtract_fusion) | copy-start | bytes 3145732
  284.3 2.6 collective-permute-start.5
  285.6 5.6 %collective-permute-start.4 = (f32[1,16,256]{2,1,0:T(8,128)S(1)}, f32[1,16,256]{2,1,0:T(8,128)S(1)}, u32[]{:S(2)}, u32[]{:S(2)}) collective-permute-start(f32[1,16,256]{2,1,0:T(8,128)S(1)} %get-tuple-element.23), channel_id=1, source_target_pairs={{4,0},{8,4},{12,8},{16,12},{20,16},{24,20},{28,24},{5,1},{9,5},{13... | collective-permute-start | bytes 49160 | tf_op jit(solution)/shard_map/ppermute | solution.py:20
  291.3 9.3 %copy-start.3 = (s32[64,16,256]{2,1,0:T(8,128)S(1)}, s32[64,16,256]{2,1,0:T(8,128)}, u32[]{:S(2)}) copy-start(s32[64,16,256]{2,1,0:T(8,128)} %param.10) | copy-start | bytes 3145732
  291.4 6.4 %collective-permute-start.6 = (f32[66,1,256]{2,0,1:T(8,128)S(1)}, f32[66,1,256]{2,0,1:T(8,128)S(1)}, u32[]{:S(2)}, u32[]{:S(2)}) collective-permute-start(f32[66,1,256]{2,0,1:T(8,128)S(1)} %copy.17), channel_id=1, source_target_pairs={{1,0},{2,1},{3,2},{5,4},{6,5},{7,6},{9,8},{10,9},{11,10},{13,12},{... | collective-permute-start | bytes 202760 | tf_op jit(solution)/shard_map/ppermute | solution.py:20
  292.8 6.5 %collective-permute-start.7 = (f32[66,1,256]{2,0,1:T(8,128)S(1)}, f32[66,1,256]{2,0,1:T(8,128)S(1)}, u32[]{:S(2)}, u32[]{:S(2)}) collective-permute-start(f32[66,1,256]{2,0,1:T(8,128)S(1)} %copy.19), channel_id=1, source_target_pairs={{0,1},{1,2},{2,3},{4,5},{5,6},{6,7},{8,9},{9,10},{10,11},{12,13},{... | collective-permute-start | bytes 202760 | tf_op jit(solution)/shard_map/ppermute | solution.py:17
  350.9 1.0 copy-start.4
  488.1 4.7 collective-permute-start.8
  492.8 6.6 %collective-permute-start.9 = (f32[8,3072]{1,0:T(8,128)S(1)}, f32[8,3072]{1,0:T(8,128)S(1)}, u32[]{:S(2)}, u32[]{:S(2)}) collective-permute-start(f32[8,3072]{1,0:T(8,128)S(1)} %add.124), channel_id=1, source_target_pairs={{0,2},{1,3},{2,0},{3,1},{4,6},{5,7},{6,4},{7,5},{8,10},{9,11},{10,... | collective-permute-start | bytes 294920 | tf_op jit(solution)/shard_map/ppermute | solution.py:93
Sparse Core Ops, SparseCore 0:
  13.5 37.6 reduce-scatter.1
  53.5 34.4 all-reduce.5
